TPU v7x, 256 devices: a whole 4x4x8 slice. The times are simulated.
256 devices in a mesh: dp: 32 (over y, x, core), seq: 8 (over z).
Axes of the slice: x: 4, y: 4, z: 8, core: 2. Of those that a mesh axis runs over, the one named last changes fastest.
Arguments:
- tokens: bfloat16 [65536, 2048], P(('dp', 'seq')), may hold values from -24 to 24
- queries: bfloat16 [65536, 1024], P(('dp', 'seq')), may hold values from -6 to 6
- kv_weight: bfloat16 [2048, 2048], P('seq'), may hold values from -0.0625 to 0.0625
- out_grad: bfloat16 [65536, 1024], P(('dp', 'seq')), may hold values from -6 to 6
Outputs:
- output: bfloat16 [65536, 1024], P(('dp', 'seq'))
- token_grad: bfloat16 [65536, 2048], P(('dp', 'seq'))
- query_grad: bfloat16 [65536, 1024], P(('dp', 'seq'))
- weight_grad: float32 [2048, 2048], P(('dp', 'seq'))
All inputs are finite; a program needn't handle non-finite values.
Results may differ from a plain program's by a relative error of at most 0.014.
Values may be sent and summed in bfloat16 or wider, within the bound.
No kernel may reach another device: no remote copies, remote signals or barrier semaphores. Data moves between devices by JAX's collectives and lax.ppermute only.
A program may use at most 128 MiB of HBM per device.

v0:
```python
import math

import jax
import jax.numpy as jnp
from jax import lax
from jax.sharding import PartitionSpec as P

HEADS = 8
HD = 128


epsilon = 1e-05


def prefix(x, axis, combine, identity, reverse):
    size, place = (lax.axis_size(axis), lax.axis_index(axis))
    everything = lax.all_gather(x, axis)
    start = jnp.broadcast_to(jnp.asarray(identity, x.dtype), x.shape)

    def lap(k, before):
        at = size - 1 - k if reverse else k
        reached = at > place if reverse else at < place
        new = combine(before, everything[at])
        return jnp.where(reached, new, before)

    return lax.fori_loop(0, size, lap, start)


def feature(inputs):
    return jnp.where(inputs > 0, inputs + 1.0, jnp.exp(jnp.minimum(inputs, 0.0)))


def feature_slope(inputs):
    return jnp.where(inputs > 0, 1.0, jnp.exp(jnp.minimum(inputs, 0.0)))


def contract(formula, first_op, second_op):
    return jnp.einsum(formula, first_op, second_op, precision=lax.Precision.HIGHEST)


def add_states(earlier, latter):
    return earlier + latter


def on_device(tokens, queries, kv_weight, out_grad):
    local_rows = tokens.shape[0]
    head_width = HEADS * HD
    weights = lax.all_gather(kv_weight, "seq", axis=0, tiled=True)
    kv_local = jnp.dot(tokens, weights, preferred_element_type=jnp.float32).astype(jnp.bfloat16)
    query_f = queries.astype(jnp.float32)
    key_f = kv_local[:, :head_width].astype(jnp.float32)
    value_f = kv_local[:, head_width:].astype(jnp.float32).reshape(local_rows, HEADS, HD)
    q_feat = feature(query_f).reshape(local_rows, HEADS, HD)
    k_feat = feature(key_f).reshape(local_rows, HEADS, HD)
    positions = jnp.arange(local_rows)
    causal = (positions[:, None] >= positions[None, :]).astype(jnp.float32)[None]
    zero_state = jnp.zeros((HEADS, HD, HD), jnp.float32)
    own_state = contract("thd,the->hde", k_feat, value_f)
    before = prefix(own_state, "seq", add_states, zero_state, False)
    scores = contract("thd,shd->hts", q_feat, k_feat) * causal
    attended = contract("hts,she->the", scores, value_f) + contract("thd,hde->the", q_feat, before)
    radius = jnp.sqrt(jnp.mean(attended * attended, axis=-1, keepdims=True) + epsilon)
    normed = attended / radius
    output = normed.astype(jnp.bfloat16).reshape(local_rows, head_width)
    grad_f = out_grad.astype(jnp.float32).reshape(local_rows, HEADS, HD)
    grad_att = (grad_f - normed * jnp.mean(grad_f * normed, axis=-1, keepdims=True)) / radius
    own_grad = contract("thd,the->hde", q_feat, grad_att)
    later_sum = prefix(own_grad, "seq", add_states, zero_state, True)
    mixed_w = contract("the,she->hts", grad_att, value_f) * causal
    grad_qf = contract("hts,shd->thd", mixed_w, k_feat) + contract("the,hde->thd", grad_att, before)
    grad_kf = contract("hts,thd->shd", mixed_w, q_feat) + contract(
        "she,hde->shd", value_f, later_sum
    )
    grad_val = contract("hts,the->she", scores, grad_att) + contract(
        "shd,hde->she", k_feat, later_sum
    )
    query_grad = (grad_qf.reshape(local_rows, head_width) * feature_slope(query_f)).astype(
        jnp.bfloat16
    )
    key_grad = (grad_kf.reshape(local_rows, head_width) * feature_slope(key_f)).astype(jnp.bfloat16)
    kv_grad = jnp.concatenate(
        [key_grad, grad_val.reshape(local_rows, head_width).astype(jnp.bfloat16)], axis=1
    )
    token_grad = lax.dot_general(
        kv_grad, weights, (((1,), (1,)), ((), ())), preferred_element_type=jnp.float32
    ).astype(jnp.bfloat16)
    batch_count = lax.axis_size("dp")
    shard_count = lax.axis_size("seq")
    grad_scale = 1.0 / math.sqrt(local_rows * batch_count * shard_count)
    weight_grad = lax.psum_scatter(
        lax.dot_general(
            tokens, kv_grad, (((0,), (0,)), ((), ())), preferred_element_type=jnp.float32
        )
        * grad_scale,
        ("dp", "seq"),
        scatter_dimension=0,
        tiled=True,
    )
    return (output, token_grad, query_grad, weight_grad)


def solution(mesh):
    in_specs = (
        P(("dp", "seq"), None),
        P(("dp", "seq"), None),
        P("seq", None),
        P(("dp", "seq"), None),
    )
    out_specs = (
        P(("dp", "seq"), None),
        P(("dp", "seq"), None),
        P(("dp", "seq"), None),
        P(("dp", "seq"), None),
    )
    return jax.shard_map(
        on_device, mesh=mesh, in_specs=in_specs, out_specs=out_specs, check_vma=False
    )
```

profile of v0, /device:TPU:0, one launch (start us, length us, event | category | flops | bytes accessed | tf_op | source)
XLA Modules:
  0.0 1618.9 jit_solution(14562147746452808177)
XLA Ops:
  7.2 0.0 all-gather.6.cloned.1.call-start
  7.2 0.7 all-gather.6.cloned.1.call-update
  7.9 0.0 all-gather.8.cloned.1.call-start
  8.0 97.2 %all-gather.6.cloned.1.call-done = bf16[2048,2048]{1,0:T(8,128)(2,1)} async-done(((bf16[256,2048]{1,0:T(8,128)(2,1)}), bf16[2048,2048]{1,0:T(8,128)(2,1)}) %all-gather.6.cloned.1.call-update) | async-done | bytes 8388624 | tf_op jit(solution)/shard_map/all_gather | solution.py:48
  105.2 5.7 convolution_convert_fusion.1
  110.9 1.4 fusion.46
  112.3 1.2 copy.67
  113.4 1.6 copy.34
  115.0 1.4 fusion.53
  116.5 0.0 all-gather.8.cloned.1.call-update
  116.5 0.0 all-gather.10.cloned.1.call-start
  116.5 2.3 copy.38
  118.8 1.3 fusion.26
  120.1 1.6 copy.64
  121.7 4.4 fusion.38
  126.1 43.9 %all-gather.8.cloned.1.call-done = f32[64,128,128]{2,1,0:T(8,128)} async-done(((f32[8,128,128]{2,1,0:T(8,128)}), f32[64,128,128]{2,1,0:T(8,128)}) %all-gather.8.cloned.1.call-update) | async-done | bytes 4194320 | tf_op jit(solution)/shard_map/all_gather | solution.py:17
  170.0 10.0 while.30
  170.0 1.2 add_select_fusion.4
  171.2 1.2 add_select_fusion.4
  172.5 1.2 add_select_fusion.4
  173.7 1.2 add_select_fusion.4
  175.0 1.2 add_select_fusion.4
  176.2 1.2 add_select_fusion.4
  177.5 1.2 add_select_fusion.4
  178.7 1.2 add_select_fusion.4
  180.0 1.0 fusion.63
  181.0 0.7 copy-done.5
  181.8 2.6 multiply_reduce_fusion.1
  184.4 0.2 multiply_reduce_fusion
  184.6 1.0 subtract_divide_fusion
  185.6 1.9 fusion.64
  187.5 0.2 reduce-scatter.4.cloned.1.call-start
  187.8 3.4 fusion.51
  191.2 49.8 %all-gather.10.cloned.1.call-done = f32[64,128,128]{2,1,0:T(8,128)} async-done(((f32[8,128,128]{2,1,0:T(8,128)}), f32[64,128,128]{2,1,0:T(8,128)}) %all-gather.10.cloned.1.call-update) | async-done | bytes 4194320 | tf_op jit(solution)/shard_map/all_gather | solution.py:17
  241.1 16.2 %while.31 = (s32[]{:T(128)}, f32[8,128,128]{2,1,0:T(8,128)}, s32[]{:T(128)}, f32[8,8,128,128]{3,2,1,0:T(8,128)}, s32[]{:T(128)}, /*index=5*/s32[]{:T(128)}, s32[]{:T(128)}, s32[]{:T(128)}) while((s32[]{:T(128)}, f32[8,128,128]{2,1,0:T(8,128)}, s32[]{:T(128)}, f32[8,8,128,128]{3,2,1,0:T(8,128)}, s32[]{:T(128)}, ...), condition=%wide.region_5.6_spmd.clone, body=%wide.region_4.5_spmd.clone.sunk | while | flops 393224 | bytes 1573027 | solution.py:26
  241.1 1.9 add_select_fusion.5
  242.9 2.0 add_select_fusion.5
  245.0 2.0 add_select_fusion.5
  247.0 2.0 add_select_fusion.5
  249.1 2.0 add_select_fusion.5
  251.1 2.0 add_select_fusion.5
  253.2 2.0 add_select_fusion.5
  255.2 2.0 add_select_fusion.5
  257.3 2.6 fusion.36
  259.9 1.6 fusion.49
  261.5 2.3 fusion.23
  263.8 2.1 copy.60
  265.8 4.3 fusion.17
  270.1 2.6 copy.59
  272.7 1.5 fusion.35
  274.3 0.8 copy-done.19
  275.1 8.1 multiply_bitcast_fusion
  283.2 17.6 %copy.62 = f32[2048,2048]{1,0:T(8,128)} copy(f32[2048,2048]{0,1:T(8,128)} %multiply_bitcast_fusion) | data formatting | bytes 33554432
  300.8 1.0 copy-done.14
  301.8 1.0 copy.52
  302.9 1.0 fusion.65
  303.9 0.6 copy-done.7
  304.4 2.3 fusion.20
  306.8 0.3 copy.61
  307.1 0.7 copy-done.18
  307.8 1.1 fusion.30
  308.9 0.0 copy-done.20
  308.9 6.9 convolution_convert_fusion
  315.7 1296.6 %reduce-scatter.4.cloned.1.call-done = f32[8,2048]{1,0:T(8,128)} async-done(((f32[2048,2048]{1,0:T(8,128)}), f32[8,2048]{1,0:T(8,128)}) %reduce-scatter.4.cloned.1.call-update) | async-done | bytes 65552
  (43 shorter events, 0.1 us)
Async XLA Ops:
  7.2 98.0 %copy-start = (bf16[256,2048]{1,0:T(8,128)(2,1)S(1)}, bf16[256,2048]{1,0:T(8,128)(2,1)}, u32[]{:S(2)}) copy-start(bf16[256,2048]{1,0:T(8,128)(2,1)} %param.8) | copy-start | bytes 3145732
  7.2 98.0 %all-gather.6.cloned.1.call-start = ((), (), s32[]{:S(2)}) async-start(), calls=%async_computation.1 | async-start | bytes 9437184 | tf_op jit(solution)/shard_map/all_gather | solution.py:48
  7.9 162.1 %all-gather.8.cloned.1.call-start = ((), (), s32[]{:S(2)}) async-start(), calls=%async_computation.2 | async-start | bytes 4718592 | tf_op jit(solution)/shard_map/all_gather | solution.py:17
  110.9 4.1 copy-start.9
  115.0 1.5 copy-start.12
  116.5 2.4 copy-start.17
  116.5 124.6 %all-gather.10.cloned.1.call-start = ((), (), s32[]{:S(2)}) async-start(), calls=%async_computation.3 | async-start | bytes 4718592 | tf_op jit(solution)/shard_map/all_gather | solution.py:17
  180.0 4.4 copy-start.2
  180.0 1.8 copy-start.5
  181.8 2.6 copy-start.8
  187.5 1424.8 %reduce-scatter.4.cloned.1.call-start = ((), (), s32[]{:S(2)}) async-start(), calls=%async_computation.4 | async-start | bytes 16842752
  257.3 2.6 copy-start.4
  257.3 2.6 copy-start.10
  257.3 4.2 copy-start.6
  270.1 2.6 copy-start.11
  272.7 2.3 copy-start.15
  274.3 0.8 copy-start.19
  300.8 1.0 copy-start.14
  300.8 2.0 copy-start.3
  300.8 3.0 copy-start.13
  302.9 1.6 copy-start.7
  306.8 1.0 copy-start.18
  306.8 2.1 copy-start.16
  307.8 1.1 copy-start.20
  308.9 1303.4 %copy-start.1 = (bf16[256,2048]{1,0:T(8,128)(2,1)S(1)}, bf16[256,2048]{1,0:T(8,128)(2,1)}, u32[]{:S(2)}) copy-start(bf16[256,2048]{1,0:T(8,128)(2,1)} %param.8) | copy-start | bytes 3145732
Sparse Core Ops, SparseCore 0:
  9.8 95.3 all-gather.5
  116.6 53.3 all-gather.7
  187.7 53.3 all-gather.9
  301.0 1311.3 reduce-scatter.3
where the time goes:
time: 1620 us
  waiting for transfers between devices  1490 us (92%)
  matrix products  49.6 us (3%)
  local copies, waits for them, and re-layouts  34 us (2%)
  other arithmetic  32.5 us (2%)
    unnamed x5, waiting for transfers between devices  1300 us
    all_gather x1, waiting for transfers between devices, on_device(): weights = lax.all_gather(kv_weight, 'seq', axis=0, tiled=True)  97.2 us
    all_gather x2, waiting for transfers between devices, prefix(): everything = lax.all_gather(x, axis)  93.7 us
  transfers between devices with their start and end apart: 4, of which 4 were waited for; matrix products, arithmetic and copies ran while one was open for 2% of the time, Pallas kernels for 0%

commit v1 on v0

v1 whole, which is shorter than its diff:
```python
import math

import jax
import jax.numpy as jnp
from jax import lax
from jax.sharding import Mesh
from jax.sharding import PartitionSpec as P

HEADS = 8
HD = 128
EPSILON = 1e-05
BF = jnp.bfloat16
F32 = jnp.float32


def feature(inputs):
    return jnp.where(inputs > 0, inputs + 1.0, jnp.exp(jnp.minimum(inputs, 0.0)))


def feature_slope(inputs):
    return jnp.where(inputs > 0, 1.0, jnp.exp(jnp.minimum(inputs, 0.0)))


def contract(formula, first_op, second_op):
    return jnp.einsum(
        formula, first_op.astype(BF), second_op.astype(BF), preferred_element_type=F32
    )


def swap_cores(x):
    return lax.ppermute(x, "core", [(0, 1), (1, 0)])


def gather_weights(kv_weight):
    rows = kv_weight.shape[0]
    planes = lax.axis_size(("y", "x", "core"))
    part = rows // planes
    mine = lax.dynamic_slice_in_dim(
        kv_weight, lax.axis_index(("y", "x", "core")) * part, part, 0
    )
    along_z = lax.all_gather(mine, "z", axis=0)
    everything = lax.all_gather(along_z, ("y", "x", "core"), axis=0)
    return everything.transpose(1, 0, 2, 3).reshape(-1, kv_weight.shape[1])


def other_shards(state, later):
    everything = lax.all_gather(state.astype(BF), "z")
    place = lax.axis_index("z")
    total = jnp.zeros(state.shape, F32)
    for k in range(lax.axis_size("z")):
        reached = k > place if later else k < place
        total = total + jnp.where(reached, everything[k].astype(F32), 0.0)
    return total.astype(BF)


def on_device(tokens, queries, kv_weight, out_grad):
    local_rows = tokens.shape[0]
    head_width = HEADS * HD
    core = lax.axis_index("core")
    by_core = tokens.reshape(local_rows, -1, 2, 64)
    kept = lax.dynamic_index_in_dim(by_core, core, 2, keepdims=False).reshape(local_rows, -1)
    sent = lax.dynamic_index_in_dim(by_core, 1 - core, 2, keepdims=False).reshape(local_rows, -1)
    chip_tokens = jnp.concatenate([kept, swap_cores(sent)], axis=0)

    weights = gather_weights(kv_weight)
    kv_local = jnp.dot(tokens, weights, preferred_element_type=F32).astype(BF)
    query_f = queries.astype(F32)
    key_f = kv_local[:, :head_width].astype(F32)
    value = kv_local[:, head_width:].reshape(local_rows, HEADS, HD)
    q_feat = feature(query_f).astype(BF).reshape(local_rows, HEADS, HD)
    k_feat = feature(key_f).astype(BF).reshape(local_rows, HEADS, HD)
    positions = jnp.arange(local_rows)
    causal = (positions[:, None] >= positions[None, :])[None]
    before = other_shards(contract("thd,the->hde", k_feat, value), False)
    scores = jnp.where(causal, contract("thd,shd->hts", q_feat, k_feat), 0.0).astype(BF)
    attended = contract("hts,she->the", scores, value) + contract("thd,hde->the", q_feat, before)
    radius = jnp.sqrt(jnp.mean(attended * attended, axis=-1, keepdims=True) + EPSILON)
    normed = attended / radius
    output = normed.astype(BF).reshape(local_rows, head_width)
    grad_f = out_grad.astype(F32).reshape(local_rows, HEADS, HD)
    grad_att = (grad_f - normed * jnp.mean(grad_f * normed, axis=-1, keepdims=True)) / radius
    grad_att = grad_att.astype(BF)
    later_sum = other_shards(contract("thd,the->hde", q_feat, grad_att), True)
    mixed_w = jnp.where(causal, contract("the,she->hts", grad_att, value), 0.0).astype(BF)
    grad_qf = contract("hts,shd->thd", mixed_w, k_feat) + contract("the,hde->thd", grad_att, before)
    grad_kf = contract("hts,thd->shd", mixed_w, q_feat) + contract(
        "she,hde->shd", value, later_sum
    )
    grad_val = contract("hts,the->she", scores, grad_att) + contract(
        "shd,hde->she", k_feat, later_sum
    )
    query_grad = (grad_qf.reshape(local_rows, head_width) * feature_slope(query_f)).astype(BF)
    key_grad = (grad_kf.reshape(local_rows, head_width) * feature_slope(key_f)).astype(BF)
    kv_grad = jnp.concatenate([key_grad, grad_val.reshape(local_rows, head_width).astype(BF)], axis=1)
    chip_grad = jnp.concatenate([kv_grad, swap_cores(kv_grad)], axis=0)
    grad_scale = 1.0 / math.sqrt(local_rows * lax.axis_size(("y", "x", "core", "z")))
    partial = lax.dot_general(
        chip_tokens, chip_grad, (((0,), (0,)), ((), ())), preferred_element_type=F32
    )
    plane = lax.psum_scatter(
        (partial * grad_scale).astype(BF), ("y", "x"), scatter_dimension=0, tiled=True
    )
    weight_grad = lax.psum_scatter(plane.astype(F32), "z", scatter_dimension=0, tiled=True)
    token_grad = lax.dot_general(
        kv_grad, weights, (((1,), (1,)), ((), ())), preferred_element_type=F32
    ).astype(BF)
    return (output, token_grad, query_grad, weight_grad)


def solution(mesh):
    shape = dict(mesh.shape)
    fine = Mesh(mesh.devices.reshape(4, shape["dp"] // 8, 2, shape["seq"]), ("y", "x", "core", "z"))
    rows = P(("y", "x", "core", "z"), None)
    return jax.shard_map(
        on_device,
        mesh=fine,
        in_specs=(rows, rows, P("z", None), rows),
        out_specs=(rows, rows, rows, rows),
        check_vma=False,
    )
```

time: 1620 us -> 341 us (0.21)
  waiting for transfers between devices: 1490 us -> 235 us
  blocking collectives: 0 us -> 28.7 us
  other arithmetic: 32.5 us -> 9.41 us
  matrix products: 49.6 us -> 29.7 us
    unnamed x5, waiting for transfers between devices: 1300 us -> 0.08 us
    reduce_scatter x0 -> x2, waiting for transfers between devices: none -> 106 us  [the longest x1 79.7 us: on_device(): lax.psum_scatter((partial * grad_scale).astype(BF), ('y', 'x'), scatter_d...]
    all_gather x3, waiting for transfers between devices: 191 us -> 128 us  [the longest x2 70.5 us: other_shards(): everything = lax.all_gather(state.astype(BF), 'z')]
    all_gather x0 -> x1, blocking collectives: none -> 28.7 us  [gather_weights(): along_z = lax.all_gather(mine, 'z', axis=0)]
    select_n x17 -> x0, other arithmetic: 27.3 us -> none  [the longest x16 26.1 us: lap(): return jnp.where(reached, new, before)]
    dot_general x14, matrix products: 42.7 us -> 22.6 us  [the longest x12 11.1 us: contract(): jnp.einsum(formula, first_op.astype(BF), second_op.astype(BF), preferred_...]
  transfers between devices with their start and end apart: 4 -> 7, of which waited for: 4 -> 6; matrix products, arithmetic and copies ran while one was open for 2% -> 7% of each run, Pallas kernels for 0% -> 0%
where the time goes in v1:
time: 341 us; the launch traced here: 339 us
  waiting for transfers between devices  235 us (69%)
  matrix products  29.7 us (9%)
  blocking collectives  28.7 us (8%)
  local copies, waits for them, and re-layouts  20.8 us (6%)
  between operations  14.1 us (4%)
  other arithmetic  9.41 us (3%)
    reduce_scatter x1, waiting for transfers between devices, on_device(): lax.psum_scatter((partial * grad_scale).astype(BF), ('y', 'x'), scatter_d...  79.7 us
    all_gather x2, waiting for transfers between devices, other_shards(): everything = lax.all_gather(state.astype(BF), 'z')  70.5 us
    all_gather x1, waiting for transfers between devices, gather_weights(): everything = lax.all_gather(along_z, ('y', 'x', 'core'), axis=0)  57.4 us
    all_gather x1, blocking collectives, gather_weights(): along_z = lax.all_gather(mine, 'z', axis=0)  28.7 us
    reduce_scatter x1, waiting for transfers between devices, on_device(): lax.psum_scatter(plane.astype(F32), 'z', scatter_dimension=0, tiled=True)  26.2 us
    unnamed x42, local copies, waits for them, and re-layouts  11.1 us
    dot_general x12, matrix products, contract(): jnp.einsum(formula, first_op.astype(BF), second_op.astype(BF), preferred_...  11.1 us
    transpose x1, local copies, waits for them, and re-layouts, gather_weights(): return everything.transpose(1, 0, 2, 3).reshape(-1, kv_weight.shape[1])  8.4 us
  transfers between devices with their start and end apart: 7, of which 6 were waited for; matrix products, arithmetic and copies ran while one was open for 7% of the time, Pallas kernels for 0%

profile of v1, /device:TPU:0, one launch (start us, length us, event | category | flops | bytes accessed | tf_op | source)
XLA Modules:
  0.0 339.1 jit_solution(5524175311786601034)
XLA Ops:
  7.2 0.0 copy-start
  7.2 0.0 all-gather.8.cloned.1.call-start
  7.2 1.2 copy-done
  8.4 28.7 %all-gather = bf16[64,2048]{1,0:T(8,128)(2,1)} all-gather(bf16[8,2048]{1,0:T(8,128)(2,1)S(1)} %constant_dynamic-slice_fusion.2), channel_id=2, replica_groups=mesh['y'=4,'x'=4,'core'=2,'z'=8] {'z'}, dimensions={0}, use_global_device_ids=true | all-gather | bytes 294912 | tf_op jit(solution)/shard_map/all_gather | solution.py:41
  37.1 0.0 all-gather.8.cloned.1.call-update
  37.1 0.0 all-gather.10.cloned.1.call-start
  37.2 57.4 %all-gather.8.cloned.1.call-done = bf16[256,8,2048]{2,1,0:T(8,128)(2,1)} async-done(((bf16[8,8,2048]{2,1,0:T(8,128)(2,1)}), bf16[256,8,2048]{2,1,0:T(8,128)(2,1)}) %all-gather.8.cloned.1.call-update) | async-done | bytes 8388624 | tf_op jit(solution)/shard_map/all_gather | solution.py:42
  94.5 8.4 %copy.59 = bf16[8,32,8,2048]{3,2,1,0:T(8,128)(2,1)} copy(bf16[8,32,8,2048]{3,2,0,1:T(8,128)(2,1)} %bitcast.99) | data formatting | bytes 16777216 | tf_op jit(solution)/shard_map/transpose | solution.py:43
  103.0 5.9 %fusion = bf16[256,2048]{0,1:T(8,128)(2,1)S(1)} fusion(bf16[2048,2048]{1,0:T(8,128)(2,1)} %bitcast.97, bf16[256,2048]{1,0:T(8,128)(2,1)S(1)} %copy-done.17), kind=kOutput, calls=%fused_computation.3 | convolution fusion | flops 2148007936 | bytes 10485760 | tf_op jit(solution)/shard_map/dot_general | solution.py:66
  108.9 0.0 copy-start.11
  108.9 0.3 fusion.15
  109.2 0.7 copy-done.11
  109.9 1.0 convolution_convert_fusion.3
  110.9 0.0 all-gather.10.cloned.1.call-update
  110.9 0.0 all-gather.12.cloned.1.call-start
  111.0 1.2 copy.60
  112.3 1.2 copy.66
  113.5 0.3 fusion.9
  113.8 0.5 select_convert_fusion.1
  114.2 0.0 copy-done.6
  114.3 0.0 copy-start.4
  114.3 1.0 copy-done.4
  115.2 1.5 fusion.31
  116.7 34.9 %all-gather.10.cloned.1.call-done = bf16[64,128,128]{2,1,0:T(8,128)(2,1)} async-done(((bf16[8,128,128]{2,1,0:T(8,128)(2,1)}), bf16[64,128,128]{2,1,0:T(8,128)(2,1)}) %all-gather.10.cloned.1.call-update) | async-done | bytes 2097168 | tf_op jit(solution)/shard_map/all_gather | solution.py:47
  151.6 2.1 fusion.24
  153.7 0.4 multiply_reduce_fusion.1
  154.1 0.2 multiply_reduce_fusion
  154.3 1.0 divide_convert_fusion
  155.3 1.0 convolution_convert_fusion.2
  156.3 0.0 all-gather.12.cloned.1.call-update
  156.3 0.0 reduce-scatter.3.cloned.1.call-start
  156.4 0.0 copy-start.5
  156.4 0.5 select_convert_fusion
  156.9 0.7 copy-done.5
  157.6 1.3 fusion.33
  158.9 1.3 fusion.32
  160.2 35.6 %all-gather.12.cloned.1.call-done = bf16[64,128,128]{2,1,0:T(8,128)(2,1)} async-done(((bf16[8,128,128]{2,1,0:T(8,128)(2,1)}), bf16[64,128,128]{2,1,0:T(8,128)(2,1)}) %all-gather.12.cloned.1.call-update) | async-done | bytes 2097168 | tf_op jit(solution)/shard_map/all_gather | solution.py:47
  195.9 2.1 fusion.23
  198.0 0.0 copy-start.12
  198.0 0.3 fusion.7
  198.4 0.3 convolution_add_fusion.2
  198.6 0.6 copy-done.12
  199.2 0.3 fusion.19
  199.5 1.1 pad_maximum_fusion
  200.6 0.0 collective-permute-start.1
  200.6 1.5 copy.74
  202.1 0.1 constant_dynamic-slice_fusion.1
  202.2 0.8 collective-permute-start
  203.0 1.5 collective-permute-done
  204.6 0.0 collective-permute-done.1
  204.6 5.6 %multiply_convert_fusion = bf16[1024,2048]{1,0:T(8,128)(2,1)} fusion(bf16[256,2048]{0,1:T(8,128)(2,1)} %collective-permute-done.1, bf16[256,1024]{0,1:T(8,128)(2,1)S(1)} %bitcast.104, bf16[256,1024]{0,1:T(8,128)(2,1)S(1)} %copy-done.16, bf16[256,1024]{0,1:T(8,128)(2,1)S(1)} %collective-permute-done, bf16[256,1024]{0,1:T(8,128)(2,1)S(1)} %bitcast.106), kind=kOutput, calls=%fused_computation | convolution fusion | flops 2160066560 | bytes 7340032 | tf_op jit(solution)/shard_map/dot_general | solution.py:97
  210.1 0.0 reduce-scatter.3.cloned.1.call-update
  210.2 0.0 reduce-scatter.5.cloned.1.call-start
  210.2 1.1 copy-done.3
  211.4 1.4 fusion.34
  212.8 79.7 %reduce-scatter.3.cloned.1.call-done = bf16[64,2048]{1,0:T(8,128)(2,1)} async-done(((bf16[1024,2048]{1,0:T(8,128)(2,1)}), bf16[64,2048]{1,0:T(8,128)(2,1)}) %reduce-scatter.3.cloned.1.call-update) | async-done | bytes 262160 | tf_op jit(solution)/shard_map/reduce_scatter | solution.py:100
  292.5 1.9 convert_element_type.168
  294.4 0.0 reduce-scatter.5.cloned.1.call-update
  294.4 1.6 convolution_add_fusion
  296.0 2.0 copy.75
  298.0 0.3 fusion.13
  298.3 1.0 copy.76
  299.3 7.1 %convolution_convert_fusion = bf16[256,2048]{1,0:T(8,128)(2,1)} fusion(bf16[2048,2048]{1,0:T(8,128)(2,1)} %bitcast.98, bf16[256,1024]{0,1:T(8,128)(2,1)} %bitcast.103, bf16[256,1024]{0,1:T(8,128)(2,1)} %copy-done.15), kind=kOutput, calls=%fused_computation.1 | convolution fusion | flops 2150105088 | bytes 10485760 | tf_op jit(solution)/shard_map/dot_general | solution.py:104
  306.4 26.2 %reduce-scatter.5.cloned.1.call-done = f32[8,2048]{1,0:T(8,128)} async-done(((f32[64,2048]{1,0:T(8,128)}), f32[8,2048]{1,0:T(8,128)}) %reduce-scatter.5.cloned.1.call-update) | async-done | bytes 65552 | tf_op jit(solution)/shard_map/reduce_scatter | solution.py:103
  (31 shorter events, 0.1 us)
Async XLA Ops:
  7.2 1.2 copy-start
  7.2 87.4 %all-gather.8.cloned.1.call-start = ((), (), s32[]{:S(2)}) async-start(), calls=%async_computation.4 | async-start | bytes 8650752 | tf_op jit(solution)/shard_map/all_gather | solution.py:42
  37.1 114.5 %all-gather.10.cloned.1.call-start = ((), (), s32[]{:S(2)}) async-start(), calls=%async_computation.5 | async-start | bytes 2359296 | tf_op jit(solution)/shard_map/all_gather | solution.py:47
  94.5 8.4 %copy-start.17 = (bf16[256,2048]{1,0:T(8,128)(2,1)S(1)}, bf16[256,2048]{1,0:T(8,128)(2,1)}, u32[]{:S(2)}) copy-start(bf16[256,2048]{1,0:T(8,128)(2,1)} %param.4) | copy-start | bytes 3145732
  108.9 1.0 copy-start.11
  109.9 2.4 copy-start.18
  110.9 85.0 %all-gather.12.cloned.1.call-start = ((), (), s32[]{:S(2)}) async-start(), calls=%async_computation.6 | async-start | bytes 2359296 | tf_op jit(solution)/shard_map/all_gather | solution.py:47
  112.3 2.0 copy-start.6
  114.3 1.0 copy-start.4
  151.6 2.1 copy-start.10
  151.6 2.5 copy-start.1
  156.3 136.2 %reduce-scatter.3.cloned.1.call-start = ((), (), s32[]{:S(2)}) async-start(), calls=%async_computation.2 | async-start | bytes 4456448 | tf_op jit(solution)/shard_map/reduce_scatter | solution.py:100
  156.4 1.2 copy-start.5
  157.6 1.3 copy-start.2
  195.9 2.1 copy-start.8
  195.9 2.4 copy-start.9
  198.0 1.2 copy-start.12
  198.3 1.2 copy-start.13
  199.5 1.1 copy-start.15
  200.6 3.9 %collective-permute-start.1 = (bf16[256,2048]{0,1:T(8,128)(2,1)}, bf16[256,2048]{0,1:T(8,128)(2,1)}, u32[]{:S(2)}, u32[]{:S(2)}) collective-permute-start(bf16[256,2048]{0,1:T(8,128)(2,1)} %pad_maximum_fusion), channel_id=1, source_target_pairs={{0,8},{8,0},{1,9},{9,1},{2,10},{10,2},{3,11},{11,3},{4,12},{12,4},... | collective-permute-start | bytes 3145736 | tf_op jit(solution)/shard_map/ppermute | solution.py:31
  202.1 2.4 copy-start.14
  202.1 2.4 copy-start.16
  202.2 2.3 collective-permute-start
  210.1 1.2 copy-start.3
  210.2 122.4 %reduce-scatter.5.cloned.1.call-start = ((), (), s32[]{:S(2)}) async-start(), calls=%async_computation.3 | async-start | bytes 589824 | tf_op jit(solution)/shard_map/reduce_scatter | solution.py:103
  294.4 3.6 %copy-start.7 = (bf16[256,1024]{0,1:T(8,128)(2,1)S(1)}, bf16[256,1024]{0,1:T(8,128)(2,1)}, u32[]{:S(2)}) copy-start(bf16[256,1024]{0,1:T(8,128)(2,1)} %copy-done.6) | copy-start | bytes 1572868
Sparse Core Ops, SparseCore 0:
  37.2 57.2 all-gather.7
  111.1 40.5 all-gather.9
  156.4 39.4 all-gather.11
  210.3 82.2 reduce-scatter.2
  295.5 37.0 reduce-scatter.4
